TPU v7x, 512 devices: a whole 4x4x16 slice. The times are simulated.
512 devices in a mesh: ctx: 64 (over x, z), ch: 8 (over y, core).
Axes of the slice: x: 4, y: 4, z: 16, core: 2. Of those that a mesh axis runs over, the one named last changes fastest.
Arguments:
- q_proj: bfloat16 [16384, 4096], P('ctx', 'ch'), may hold values from -6 to 6
- k_proj: bfloat16 [16384, 4096], P('ctx', 'ch'), may hold values from -6 to 6
- v_proj: bfloat16 [16384, 4096], P('ctx', 'ch'), may hold values from -6 to 6
- residue: float32 [16, 4096], P(None, 'ch'), may hold values from -4 to 4
- rate: float32 [16, 4096], P(None, 'ch'), may hold values from 1.2207031e-05 to 0.1
- skip: float32 [4096], P('ch'), may hold values from -4 to 4
- w_out: bfloat16 [4096, 6144], P('ctx', 'ch'), may hold values from -0.09375 to 0.09375
Outputs:
- mixed: bfloat16 [16384, 6144], P('ctx', 'ch')
All inputs are finite; a program needn't handle non-finite values.
Results may differ from a plain program's by a relative error of at most 0.0049.
Values may be sent and summed in bfloat16 or wider, within the bound.
A program may use at most 128 MiB of HBM per device.

v0:
```python
import jax
import jax.numpy as jnp
from jax import lax
from jax.sharding import PartitionSpec as P


def carried_in(part, axis, combine, identity):
    place = lax.axis_index(axis)
    gathered = jax.tree.map(lambda a: lax.all_gather(a, axis), part)
    state = jax.tree.map(lambda a, e: jnp.zeros_like(a) + jnp.asarray(e, a.dtype), part, identity)

    def one(turn, state):
        return combine(
            state, jax.tree.map(lambda a: lax.dynamic_index_in_dim(a, turn, 0, False), gathered)
        )

    return lax.fori_loop(0, place, one, state)


def compose(earlier, later):
    return (earlier[0] * later[0], later[0] * earlier[1] + later[1])


def body(q_proj, k_proj, v_proj, residue, rate, skip, w_out):
    highest = lax.Precision.HIGHEST
    tok_rows, chan_count = q_proj.shape
    signal = k_proj.astype(jnp.float32) * v_proj.astype(jnp.float32)
    sub_len = min(64, tok_rows // 4)
    sub_count = tok_rows // sub_len
    pieces = signal.reshape(sub_count, sub_len, chan_count)
    lag_steps = jnp.arange(sub_len).astype(jnp.float32)
    powers = jnp.exp(-rate[:, None, :] * lag_steps[None, :, None])
    coefficient = residue * jnp.sqrt(2.0 * rate)
    filter_taps = jnp.einsum("mc,mkc->kc", coefficient, powers, precision=highest)
    offsets = jnp.arange(sub_len)[:, None] - jnp.arange(sub_len)[None, :]
    toeplitz = jnp.where(
        (offsets >= 0)[:, :, None], filter_taps[jnp.clip(offsets, 0, sub_len - 1)], 0.0
    )
    local_part = jnp.einsum("tsc,bsc->btc", toeplitz, pieces, precision=highest)
    ends = jnp.einsum("msc,bsc->bmc", powers[:, ::-1, :], pieces, precision=highest)
    sub_index = jnp.arange(sub_count)
    sub_gap = sub_index[:, None] - 1 - sub_index[None, :]
    gap_float = jnp.maximum(sub_gap, 0).astype(jnp.float32)
    within = jnp.where(
        (sub_gap >= 0)[:, :, None, None],
        jnp.exp(-(rate * sub_len)[None, None] * gap_float[:, :, None, None]),
        0.0,
    )
    inner = jnp.einsum("bamc,amc->bmc", within, ends, precision=highest)
    sub_decay = jnp.exp(-rate * sub_len)
    total_end = sub_decay * inner[-1] + ends[-1]
    dev_decay = jnp.exp(-rate * tok_rows)
    prefix = carried_in(
        (dev_decay, total_end),
        "ctx",
        compose,
        (jnp.ones_like(dev_decay), jnp.zeros_like(total_end)),
    )
    entering = prefix[1]
    start_powers = jnp.exp(-(rate * sub_len)[None] * sub_index.astype(jnp.float32)[:, None, None])
    arriving = inner + start_powers * entering[None]
    reach = coefficient[:, None, :] * powers * jnp.exp(-rate)[:, None, :]
    carried = jnp.einsum("mtc,bmc->btc", reach, arriving, precision=highest)
    conv = (local_part + carried).reshape(tok_rows, chan_count) + skip[None, :] * signal
    gated = (q_proj.astype(jnp.float32) * conv).astype(jnp.bfloat16)
    full_gated = lax.all_gather(gated, "ch", axis=1, tiled=True)
    mixed = jnp.dot(
        full_gated,
        lax.all_gather(w_out, "ctx", axis=0, tiled=True),
        preferred_element_type=jnp.float32,
    )
    return mixed.astype(jnp.bfloat16)


def solution(mesh):
    placed = (
        P("ctx", "ch"),
        P("ctx", "ch"),
        P("ctx", "ch"),
        P(None, "ch"),
        P(None, "ch"),
        P("ch"),
        P("ctx", "ch"),
    )
    return jax.shard_map(
        body, mesh=mesh, in_specs=placed, out_specs=P("ctx", "ch"), check_vma=False
    )
```

profile of v0, /device:TPU:32, one launch (start us, length us, event | category | flops | bytes accessed | tf_op | source)
XLA Modules:
  0.0 568.6 jit_solution(16598735904272384695)
XLA Ops:
  6.7 1.1 convert_multiply_fusion
  7.8 0.4 copy.49
  8.2 0.8 multiply_negate_fusion
  9.0 0.1 copy.47
  9.1 3.6 multiply_exponential_fusion
  12.7 7.3 %rev.3 = f32[16,64,512]{1,0,2:T(8,128)} reverse(f32[16,64,512]{1,0,2:T(8,128)} %multiply_exponential_fusion), dimensions={1} | reverse | bytes 4194304 | tf_op jit(solution)/shard_map/rev | solution.py:40
  20.0 8.4 %fusion.23 = f32[512,4,16]{2,1,0:T(4,128)S(1)} fusion(f32[4,64,512]{1,0,2:T(4,128)S(1)} %copy.49, f32[16,64,512]{1,0,2:T(8,128)} %rev.3), kind=kOutput, calls=%fused_computation.43 | convolution fusion | flops 25165824 | bytes 2752512 | tf_op jit(solution)/shard_map/msc,bsc->bmc/dot_general | solution.py:40
  28.3 0.3 copy.73
  28.6 0.2 multiply_reduce_fusion.1
  28.9 0.7 negate_exponential_fusion
  29.6 0.7 all-gather.13.cloned.1.call-update
  30.3 0.2 all-gather.7.cloned.1.call-start
  30.5 0.8 copy.52
  31.4 0.1 copy.71
  31.5 6.0 %multiply_reduce_fusion = f32[512,64]{1,0:T(8,128)S(1)} fusion(f32[512,16]{1,0:T(8,128)S(1)} %copy.71, f32[64]{0:T(128)S(1)} %iota_convert_fusion.1, f32[16,512]{0,1:T(8,128)S(1)} %copy.47), kind=kLoop, calls=%fused_computation.7 | loop fusion | flops 1540096 | bytes 196864
  37.5 0.1 copy.61
  37.7 16.8 %gather_fusion = f32[4096,512]{1,0:T(8,128)} fusion(f32[64,512]{1,0:T(8,128)S(1)} %bitcast.54, s32[4096]{0:T(1024)S(1)} %broadcast_clamp_fusion), kind=kCustom, calls=%fused_computation | custom fusion | bytes 16793600 | tf_op jit(solution)/shard_map/gather | solution.py:37
  54.5 16.3 %copy.48 = f32[64,64,512]{1,0,2:T(8,128)} copy(f32[64,64,512]{2,1,0:T(8,128)} %bitcast.55) | data formatting | bytes 16777216 | tf_op jit(solution)/shard_map/gather | solution.py:37
  70.8 0.8 copy.53
  71.7 29.0 %fusion = f32[512,4,64]{2,1,0:T(4,128)S(1)} fusion(f32[4,64,512]{1,0,2:T(4,128)S(1)} %copy.49, f32[64,64,512]{1,0,2:T(8,128)} %copy.48, pred[64,64]{1,0:T(8,128)(4,1)S(1)} %subtract_compare_fusion), kind=kOutput, calls=%fused_computation.3 | convolution fusion | flops 102760448 | bytes 9441280 | tf_op jit(solution)/shard_map/tsc,bsc->btc/dot_general | solution.py:39
  100.7 74.2 %all-gather.11.cloned.1.call-done = f32[1024,512]{1,0:T(8,128)} async-done(((f32[16,512]{1,0:T(8,128)}), f32[1024,512]{1,0:T(8,128)}) %all-gather.11.cloned.1.call-update) | async-done | bytes 2097168 | tf_op jit(solution)/shard_map/all_gather | solution.py:9
  174.9 139.8 %all-gather.13.cloned.1.call-done = f32[1024,512]{1,0:T(8,128)} async-done(((f32[16,512]{1,0:T(8,128)}), f32[1024,512]{1,0:T(8,128)}) %all-gather.13.cloned.1.call-update) | async-done | bytes 2097168 | tf_op jit(solution)/shard_map/all_gather | solution.py:9
  314.7 0.8 while.12
  314.7 0.8 bitcast_add_fusion.3
  315.6 0.4 copy.54
  316.0 8.4 %fusion.14 = f32[4,64,512]{1,0,2:T(4,128)S(1)} fusion(f32[512,4,64]{2,1,0:T(4,128)S(1)} %fusion, f32[4,16,512]{1,0,2:T(4,128)S(1)} %copy.54, f32[16,512]{0,1:T(8,128)} %copy.53, f32[16,512]{0,1:T(8,128)} %copy.52, f32[64]{0:T(128)S(1)} %iota_convert_fusion.1, f32[16,512]{0,1:T(8,128)S(1)} %copy.47), kind=kOutput, calls=%fused_computation.17 | convolution fusion | flops 26869760 | bytes 1278208 | tf_op jit(solution)/shard_map/mtc,bmc->btc/dot_general | solution.py:63
  324.5 0.3 copy.55
  324.9 2.0 fusion.18
  326.9 0.5 all-gather.9.cloned.1.call-update
  327.4 74.4 %all-gather.7.cloned.1.call-done = bf16[256,4096]{1,0:T(8,128)(2,1)} async-done(((bf16[256,512]{1,0:T(8,128)(2,1)}), bf16[256,4096]{1,0:T(8,128)(2,1)}) %all-gather.7.cloned.1.call-update) | async-done | bytes 2097168 | tf_op jit(solution)/shard_map/all_gather | solution.py:66
  401.8 154.3 %all-gather.9.cloned.1.call-done = bf16[4096,768]{1,0:T(8,128)(2,1)} async-done(((bf16[64,768]{1,0:T(8,128)(2,1)}), bf16[4096,768]{1,0:T(8,128)(2,1)}) %all-gather.9.cloned.1.call-update) | async-done | bytes 6291472 | tf_op jit(solution)/shard_map/all_gather | solution.py:69
  556.2 6.0 %convolution_convert_fusion = bf16[256,768]{1,0:T(8,128)(2,1)} fusion(bf16[256,4096]{1,0:T(8,128)(2,1)} %all-gather.7.cloned.1.call-done, bf16[4096,768]{1,0:T(8,128)(2,1)} %all-gather.9.cloned.1.call-done), kind=kOutput, calls=%fused_computation.18 | convolution fusion | flops 1610809344 | bytes 8781824 | tf_op jit(solution)/shard_map/dot_general | solution.py:67
  (22 shorter events, 0.5 us)
Async XLA Ops:
  6.5 168.4 %all-gather.11.cloned.1.call-start = ((), (), s32[]{:S(2)}) async-start(), calls=%async_computation.2 | async-start | bytes 2129920 | tf_op jit(solution)/shard_map/all_gather | solution.py:9
  20.0 8.9 %copy-start = (f32[16,512]{1,0:T(8,128)S(1)}, f32[16,512]{1,0:T(8,128)}, u32[]{:S(2)}) copy-start(f32[16,512]{1,0:T(8,128)} %param.13) | copy-start | bytes 98308
  20.0 8.9 %copy-start.1 = (f32[16,512]{1,0:T(8,128)S(1)}, f32[16,512]{1,0:T(8,128)}, u32[]{:S(2)}) copy-start(f32[16,512]{1,0:T(8,128)} %param.12) | copy-start | bytes 98308
  29.5 285.2 %all-gather.13.cloned.1.call-start = ((), (), s32[]{:S(2)}) async-start(), calls=%async_computation.3 | async-start | bytes 2129920 | tf_op jit(solution)/shard_map/all_gather | solution.py:9
  30.3 371.5 %all-gather.7.cloned.1.call-start = ((), (), s32[]{:S(2)}) async-start(), calls=%async_computation | async-start | bytes 2359296 | tf_op jit(solution)/shard_map/all_gather | solution.py:66
  316.0 8.8 %copy-start.2 = (f32[512]{0:T(512)S(1)}, f32[512]{0:T(512)}, u32[]{:S(2)}) copy-start(f32[512]{0:T(512)} %param.14) | copy-start | bytes 6148
  326.8 229.3 %all-gather.9.cloned.1.call-start = ((), (), s32[]{:S(2)}) async-start(), calls=%async_computation.1 | async-start | bytes 6389760 | tf_op jit(solution)/shard_map/all_gather | solution.py:69
Sparse Core Ops, SparseCore 0:
  29.7 145.1 all-gather.10
  177.8 136.8 all-gather.12
  326.9 74.8 all-gather.6
  404.6 151.4 all-gather.8
where the time goes:
time: 574 us; the launch traced here: 569 us
  waiting for transfers between devices  444 us (77%)
  matrix products  51.7 us (9%)
  local copies, waits for them, and re-layouts  44 us (8%)
  other arithmetic  15.3 us (3%)
  between operations  13.3 us (2%)
    all_gather x2, waiting for transfers between devices, carried_in(): gathered = jax.tree.map(lambda a: lax.all_gather(a, axis), part)  214 us
    all_gather x1, waiting for transfers between devices, body(): lax.all_gather(w_out, 'ctx', axis=0, tiled=True)  154 us
    all_gather x1, waiting for transfers between devices, body(): full_gated = lax.all_gather(gated, 'ch', axis=1, tiled=True)  74.4 us
    gather x2, local copies, waits for them, and re-layouts, body(): filter_taps[jnp.clip(offsets, 0, sub_len - 1)]  33.1 us
    dot_general x1, matrix products, body(): local_part = jnp.einsum('tsc,bsc->btc', toeplitz, pieces, precision=highest)  29 us
  transfers between devices with their start and end apart: 4, of which 4 were waited for; matrix products, arithmetic and copies ran while one was open for 12% of the time, Pallas kernels for 0%

commit v1 on v0

--- a/solution.py
+++ b/solution.py
@@ -2,6 +2,11 @@
 import jax.numpy as jnp
 from jax import lax
 from jax.sharding import PartitionSpec as P
+
+
+def exchange_gather(array, name, d):
+    outgoing = jnp.stack([array] * lax.axis_size(name))
+    return jnp.concatenate(lax.all_to_all(outgoing, name, 0, 0), axis=d)
 
 
 def carried_in(part, axis, combine, identity):
@@ -65,9 +70,7 @@
     gated = (q_proj.astype(jnp.float32) * conv).astype(jnp.bfloat16)
     full_gated = lax.all_gather(gated, "ch", axis=1, tiled=True)
     mixed = jnp.dot(
-        full_gated,
-        lax.all_gather(w_out, "ctx", axis=0, tiled=True),
-        preferred_element_type=jnp.float32,
+        full_gated, exchange_gather(w_out, "ctx", 0), preferred_element_type=jnp.float32
     )
     return mixed.astype(jnp.bfloat16)
 

time: 574 us -> 497 us (0.87)
  the two profiles are of different devices: /device:TPU:32 before, /device:TPU:1 now
where the time goes in v1:
time: 497 us; the launch traced here: 492 us
  waiting for transfers between devices  346 us (70%)
  matrix products  51.7 us (10%)
  local copies, waits for them, and re-layouts  48.2 us (10%)
  starting transfers between devices  19.8 us (4%)
  between operations  13.3 us (3%)
  other arithmetic  12.7 us (3%)
    all_gather x2, waiting for transfers between devices, carried_in(): gathered = jax.tree.map(lambda a: lax.all_gather(a, axis), part)  259 us
    all_gather x1, waiting for transfers between devices, body(): full_gated = lax.all_gather(gated, 'ch', axis=1, tiled=True)  86.3 us
    gather x2, local copies, waits for them, and re-layouts, body(): filter_taps[jnp.clip(offsets, 0, sub_len - 1)]  33 us
    dot_general x1, matrix products, body(): local_part = jnp.einsum('tsc,bsc->btc', toeplitz, pieces, precision=highest)  29 us
    all_to_all x1, starting transfers between devices, exchange_gather(): return jnp.concatenate(lax.all_to_all(outgoing, name, 0, 0), axis=d)  19.5 us
  transfers between devices with their start and end apart: 4, of which 3 were waited for; matrix products, arithmetic and copies ran while one was open for 21% of the time, Pallas kernels for 0%

profile of v1, /device:TPU:1, one launch (start us, length us, event | category | flops | bytes accessed | tf_op | source)
XLA Modules:
  0.0 492.0 jit_solution(16667361858153339948)
XLA Ops:
  6.5 4.4 stack.2
  10.9 19.5 %all-to-all-start = ((bf16[64,64,768]{2,1,0:T(8,128)(2,1)}), bf16[64,64,768]{2,1,0:T(8,128)(2,1)}, u32[]{:S(2)}, u32[]{:S(2)}) async-start(bf16[64,64,768]{2,1,0:T(8,128)(2,1)} %stack.2), calls=%async_computation | async-start | bytes 12582912 | tf_op jit(solution)/shard_map/all_to_all | solution.py:9
  30.5 0.4 copy.49
  31.0 0.1 copy.47
  31.1 3.6 multiply_exponential_fusion
  34.7 7.3 %rev.3 = f32[16,64,512]{1,0,2:T(8,128)} reverse(f32[16,64,512]{1,0,2:T(8,128)} %multiply_exponential_fusion), dimensions={1} | reverse | bytes 4194304 | tf_op jit(solution)/shard_map/rev | solution.py:45
  41.9 8.4 %fusion.23 = f32[512,4,16]{2,1,0:T(4,128)S(1)} fusion(f32[4,64,512]{1,0,2:T(4,128)S(1)} %copy.49, f32[16,64,512]{1,0,2:T(8,128)} %rev.3), kind=kOutput, calls=%fused_computation.43 | convolution fusion | flops 25165824 | bytes 2752512 | tf_op jit(solution)/shard_map/msc,bsc->bmc/dot_general | solution.py:45
  50.3 0.3 copy.73
  50.6 0.1 fusion.21
  50.7 0.1 maximum_convert_fusion
  50.8 0.2 multiply_reduce_fusion.1
  51.0 0.6 negate_exponential_fusion
  51.7 0.7 all-gather.10.cloned.1.call-update
  52.4 0.2 all-gather.6.cloned.1.call-start
  52.6 0.8 copy.52
  53.5 0.1 copy.71
  53.6 6.0 %multiply_reduce_fusion = f32[512,64]{1,0:T(8,128)S(1)} fusion(f32[512,16]{1,0:T(8,128)S(1)} %copy.71, f32[64]{0:T(128)S(1)} %iota_convert_fusion.1, f32[16,512]{0,1:T(8,128)S(1)} %copy.47), kind=kLoop, calls=%fused_computation.7 | loop fusion | flops 1540096 | bytes 196864
  59.6 0.1 copy.61
  59.7 0.1 reshape.118
  59.8 16.8 %gather_fusion = f32[4096,512]{1,0:T(8,128)} fusion(f32[64,512]{1,0:T(8,128)S(1)} %bitcast.55, s32[4096]{0:T(1024)S(1)} %broadcast_clamp_fusion), kind=kCustom, calls=%fused_computation | custom fusion | bytes 16793600 | tf_op jit(solution)/shard_map/gather | solution.py:42
  76.6 16.2 %copy.48 = f32[64,64,512]{1,0,2:T(8,128)} copy(f32[64,64,512]{2,1,0:T(8,128)} %bitcast.56) | data formatting | bytes 16777216 | tf_op jit(solution)/shard_map/gather | solution.py:42
  92.8 0.8 copy.53
  93.7 29.0 %fusion = f32[512,4,64]{2,1,0:T(4,128)S(1)} fusion(f32[4,64,512]{1,0,2:T(4,128)S(1)} %copy.49, f32[64,64,512]{1,0,2:T(8,128)} %copy.48, pred[64,64]{1,0:T(8,128)(4,1)S(1)} %subtract_compare_fusion), kind=kOutput, calls=%fused_computation.3 | convolution fusion | flops 102760448 | bytes 9441280 | tf_op jit(solution)/shard_map/tsc,bsc->btc/dot_general | solution.py:44
  122.6 103.9 %all-gather.8.cloned.1.call-done = f32[1024,512]{1,0:T(8,128)} async-done(((f32[16,512]{1,0:T(8,128)}), f32[1024,512]{1,0:T(8,128)}) %all-gather.8.cloned.1.call-update) | async-done | bytes 2097168 | tf_op jit(solution)/shard_map/all_gather | solution.py:14
  226.5 155.3 %all-gather.10.cloned.1.call-done = f32[1024,512]{1,0:T(8,128)} async-done(((f32[16,512]{1,0:T(8,128)}), f32[1024,512]{1,0:T(8,128)}) %all-gather.10.cloned.1.call-update) | async-done | bytes 2097168 | tf_op jit(solution)/shard_map/all_gather | solution.py:14
  381.8 0.1 multiply_add_fusion
  381.9 0.4 copy.54
  382.3 8.4 %fusion.14 = f32[4,64,512]{1,0,2:T(4,128)S(1)} fusion(f32[512,4,64]{2,1,0:T(4,128)S(1)} %fusion, f32[4,16,512]{1,0,2:T(4,128)S(1)} %copy.54, f32[16,512]{0,1:T(8,128)} %copy.53, f32[16,512]{0,1:T(8,128)} %copy.52, f32[64]{0:T(128)S(1)} %iota_convert_fusion.1, f32[16,512]{0,1:T(8,128)S(1)} %copy.47), kind=kOutput, calls=%fused_computation.17 | convolution fusion | flops 26869760 | bytes 1278208 | tf_op jit(solution)/shard_map/mtc,bmc->btc/dot_general | solution.py:68
  390.8 0.3 copy.55
  391.1 2.0 fusion.18
  393.1 86.3 %all-gather.6.cloned.1.call-done = bf16[256,4096]{1,0:T(8,128)(2,1)} async-done(((bf16[256,512]{1,0:T(8,128)(2,1)}), bf16[256,4096]{1,0:T(8,128)(2,1)}) %all-gather.6.cloned.1.call-update) | async-done | bytes 2097168 | tf_op jit(solution)/shard_map/all_gather | solution.py:71
  479.5 6.0 %convolution_convert_fusion = bf16[256,768]{1,0:T(8,128)(2,1)} fusion(bf16[256,4096]{1,0:T(8,128)(2,1)} %all-gather.6.cloned.1.call-done, bf16[4096,768]{1,0:T(8,128)(2,1)} %bitcast.20), kind=kOutput, calls=%fused_computation.18 | convolution fusion | flops 1610809344 | bytes 8781824 | tf_op jit(solution)/shard_map/dot_general | solution.py:72
  (25 shorter events, 0.3 us)
Async XLA Ops:
  10.9 19.5 %copy-start = (bf16[256,512]{1,0:T(8,128)(2,1)S(1)}, bf16[256,512]{1,0:T(8,128)(2,1)}, u32[]{:S(2)}) copy-start(bf16[256,512]{1,0:T(8,128)(2,1)} %param.11) | copy-start | bytes 786436
  10.9 19.5 %copy-start.1 = (bf16[256,512]{1,0:T(8,128)(2,1)S(1)}, bf16[256,512]{1,0:T(8,128)(2,1)}, u32[]{:S(2)}) copy-start(bf16[256,512]{1,0:T(8,128)(2,1)} %param.10) | copy-start | bytes 786436
  10.9 20.0 %copy-start.2 = (f32[16,512]{1,0:T(8,128)S(1)}, f32[16,512]{1,0:T(8,128)}, u32[]{:S(2)}) copy-start(f32[16,512]{1,0:T(8,128)} %param.13) | copy-start | bytes 98308
  10.9 468.5 %all-to-all-start = ((bf16[64,64,768]{2,1,0:T(8,128)(2,1)}), bf16[64,64,768]{2,1,0:T(8,128)(2,1)}, u32[]{:S(2)}, u32[]{:S(2)}) async-start(bf16[64,64,768]{2,1,0:T(8,128)(2,1)} %stack.2), calls=%async_computation | async-start | bytes 12582912 | tf_op jit(solution)/shard_map/all_to_all | solution.py:9
  30.4 196.1 %all-gather.8.cloned.1.call-start = ((), (), s32[]{:S(2)}) async-start(), calls=%async_computation.2 | async-start | bytes 2129920 | tf_op jit(solution)/shard_map/all_gather | solution.py:14
  41.9 9.1 %copy-start.3 = (f32[16,512]{1,0:T(8,128)S(1)}, f32[16,512]{1,0:T(8,128)}, u32[]{:S(2)}) copy-start(f32[16,512]{1,0:T(8,128)} %param.12) | copy-start | bytes 98308
  51.7 330.2 %all-gather.10.cloned.1.call-start = ((), (), s32[]{:S(2)}) async-start(), calls=%async_computation.3 | async-start | bytes 2129920 | tf_op jit(solution)/shard_map/all_gather | solution.py:14
  52.4 427.1 %all-gather.6.cloned.1.call-start = ((), (), s32[]{:S(2)}) async-start(), calls=%async_computation.1 | async-start | bytes 2359296 | tf_op jit(solution)/shard_map/all_gather | solution.py:71
  382.3 8.8 %copy-start.4 = (f32[512]{0:T(512)S(1)}, f32[512]{0:T(512)}, u32[]{:S(2)}) copy-start(f32[512]{0:T(512)} %param.14) | copy-start | bytes 6148
Sparse Core Ops, SparseCore 0:
  51.8 174.6 all-gather.7
  229.4 152.3 all-gather.9
  393.2 86.1 all-gather.5
